TPU v7x, 32 devices: a whole 2x2x4 slice. The times are simulated.
32 devices in a mesh: chaos: 4 (over z), gx: 4 (over y, x), gy: 2 (over core).
Axes of the slice: x: 2, y: 2, z: 4, core: 2. Of those that a mesh axis runs over, the one named last changes fastest.
Arguments:
- lam_start: float32 [286, 16, 512], P(None, ('chaos', 'gy'), 'gx'), may hold values from -6 to 6
- adj_source: float32 [286, 16, 512], P(None, ('chaos', 'gy'), 'gx'), may hold values from -6 to 6
- coef_points: float32 [512, 4, 4, 512], P('chaos', None, 'gy', 'gx'), may hold values from 0.1 to 1
- quad_index: int32 [512, 10], replicated, may hold values from 0 to 3
- mode_index: int32 [286, 10], replicated, may hold values from 0 to 3, as said below
Outputs:
- lam_end: float32 [286, 16, 512], P(None, ('chaos', 'gy'), 'gx')
Inputs may be any that keep to these rules, and one draw needn't show every extreme that they name: `mode_index`: each row is a multi-index whose degrees sum to at most 3; each such multi-index of 10 inputs appears exactly once.
All inputs are finite; a program needn't handle non-finite values.
Results may differ from a plain program's by a relative error of at most 0.00011.
Values sent between devices are 32-bit elements; how exact they have to be, the bound alone decides.
A program may use at most 64 MiB of HBM per device.

v0:
```python
import math
import jax
import jax.numpy as jnp
from jax import lax
from jax.sharding import PartitionSpec as P

STEPS = 2
gauss_nodes = (-2.3344142183389773, -0.7419637843027259, 0.7419637843027259, 2.3344142183389773)
gauss_weights = (0.04587585476806849, 0.4541241452319315, 0.4541241452319315, 0.04587585476806849)
mass_shift = 1.0
relax_rate = 0.2
top_prec = lax.Precision.HIGHEST


def tables(quad_index, mode_index):
    node_vals = jnp.array(gauss_nodes, jnp.float32)
    node_wts = jnp.array(gauss_weights, jnp.float32)
    hermite = jnp.stack(
        [
            jnp.ones_like(node_vals),
            node_vals,
            (node_vals * node_vals - 1.0) / math.sqrt(2.0),
            (node_vals * node_vals * node_vals - 3.0 * node_vals) / math.sqrt(6.0),
        ],
        0,
    )
    levels = jnp.arange(4, dtype=jnp.int32)
    quad_hot = (quad_index[:, :, None] == levels[None, None, :]).astype(jnp.float32)
    mode_hot = (mode_index[:, :, None] == levels[None, None, :]).astype(jnp.float32)
    at_nodes = jnp.einsum("qdk,nk->qdn", quad_hot, hermite, precision=top_prec)
    factors = jnp.einsum("qdn,pdn->qpd", at_nodes, mode_hot, precision=top_prec)
    chaos_basis = jnp.prod(factors, axis=2)
    point_wts = jnp.prod(jnp.sum(quad_hot * node_wts[None, None, :], axis=2), axis=1)
    point_wts = point_wts / jnp.sum(point_wts)
    back_map = chaos_basis * point_wts[:, None]
    return (chaos_basis, back_map)


def shift_pair(low, high, axis):
    size = lax.axis_size(axis)
    up = [(i, (i + 1) % size) for i in range(size)]
    down = [(j, i) for i, j in up]
    return (lax.ppermute(high, axis, up), lax.ppermute(low, axis, down))


def local(lam_start, adj_source, coef_points, quad_index, mode_index):
    modes, row_len, col_len = lam_start.shape
    points = quad_index.shape[0]
    rows = ("chaos", "gy")
    row_dev = lax.axis_index(rows)
    row_devs = lax.axis_size(rows)
    keep_low = jnp.where(row_dev == 0, 0.0, 1.0).astype(jnp.float32)
    keep_high = jnp.where(row_dev == row_devs - 1, 0.0, 1.0).astype(jnp.float32)
    coef = lax.all_to_all(coef_points, "chaos", split_axis=1, concat_axis=0, tiled=True)
    coef = coef.reshape(points, row_len, col_len)
    k_low, k_high = shift_pair(coef[:, 0], coef[:, -1], rows)
    k_left, k_right = shift_pair(coef[:, :, :1], coef[:, :, -1:], "gx")
    chaos_basis, back_map = tables(quad_index, mode_index)
    coef_y = [k_low * keep_low] + [coef[:, r] for r in range(row_len)] + [k_high * keep_high]
    coef_x = [jnp.concatenate([k_left[:, r], coef[:, r], k_right[:, r]], 1) for r in range(row_len)]
    lam_now = lam_start
    for repeat in range(STEPS):
        v_low, v_high = shift_pair(lam_now[:, :2], lam_now[:, -2:], rows)
        v_left, v_right = shift_pair(lam_now[:, :, :2], lam_now[:, :, -2:], "gx")
        v_low = v_low * keep_low
        v_high = v_high * keep_high
        parts = (
            [v_low[:, 0], v_low[:, 1]]
            + [lam_now[:, r] for r in range(row_len)]
            + [v_high[:, 0], v_high[:, 1]]
        )
        edges = [v_left[:, r] for r in range(row_len)] + [v_right[:, r] for r in range(row_len)]
        u = jnp.dot(
            chaos_basis,
            jnp.concatenate(parts + edges, 1),
            precision=top_prec,
            preferred_element_type=jnp.float32,
        )
        u_row = [u[:, i * col_len : (i + 1) * col_len] for i in range(row_len + 4)]
        base = (row_len + 4) * col_len
        u_left = [u[:, base + 2 * r : base + 2 * r + 2] for r in range(row_len)]
        base += 2 * row_len
        u_right = [u[:, base + 2 * r : base + 2 * r + 2] for r in range(row_len)]
        flux_y = [coef_y[i] * ((u_row[i + 2] - u_row[i]) * 0.5) for i in range(row_len + 2)]
        div = []
        for r in range(row_len):
            wide = jnp.concatenate([u_left[r], u_row[r + 2], u_right[r]], 1)
            flux_x = coef_x[r] * ((wide[:, 2:] - wide[:, :-2]) * 0.5)
            div.append((flux_x[:, 2:] - flux_x[:, :-2]) * 0.5 + (flux_y[r + 2] - flux_y[r]) * 0.5)
        back = jnp.dot(
            back_map.T,
            jnp.concatenate(div, 1),
            precision=top_prec,
            preferred_element_type=jnp.float32,
        )
        divergence = back.reshape(modes, row_len, col_len)
        lam_now = lam_now + relax_rate * (adj_source - (mass_shift * lam_now - divergence))
    return lam_now


def solution(mesh):
    placed = (
        P(None, ("chaos", "gy"), "gx"),
        P(None, ("chaos", "gy"), "gx"),
        P("chaos", None, "gy", "gx"),
        P(),
        P(),
    )
    return jax.shard_map(
        local, mesh=mesh, in_specs=placed, out_specs=P(None, ("chaos", "gy"), "gx"), check_vma=False
    )
```

profile of v0, /device:TPU:0, one launch (start us, length us, event | category | flops | bytes accessed | tf_op | source)
XLA Modules:
  0.0 80.5 jit_solution(6977557665041020564)
XLA Ops:
  0.0 1.0 %copy.78 = f32[286,2,128]{2,0,1:T(8,128)S(1)} copy(f32[286,2,128]{2,1,0:T(2,128)} %param.7) | data formatting | bytes 585728 | tf_op args[0]
  1.0 4.5 %collective-permute-start.3 = (f32[286,2,128]{2,0,1:T(8,128)S(1)}, f32[286,2,128]{2,0,1:T(8,128)S(1)}, u32[]{:S(2)}, u32[]{:S(2)}) collective-permute-start(f32[286,2,128]{2,0,1:T(8,128)S(1)} %copy.78), channel_id=1, source_target_pairs={{1,0},{8,1},{9,8},{16,9},{17,16},{24,17},{25,24},{0,25},{3,2},{10,... | collective-permute-start | bytes 878600 | tf_op jit(solution)/shard_map/ppermute | solution.py:43
  5.5 2.0 %copy.67 = f32[128,4,2,128]{3,2,0,1:T(2,128)} copy(f32[128,4,2,128]{3,2,1,0:T(2,128)} %param.9) | data formatting | bytes 1048576 | tf_op args[2]
  7.6 3.6 %all-to-all-start = ((f32[128,4,2,128]{3,2,0,1:T(2,128)}), f32[128,4,2,128]{3,2,0,1:T(2,128)S(1)}, u32[]{:S(2)}, u32[]{:S(2)}) async-start(f32[128,4,2,128]{3,2,0,1:T(2,128)} %copy.67), calls=%async_computation | async-start | bytes 1048576 | tf_op jit(solution)/shard_map/all_to_all | solution.py:54
  11.2 0.1 fusion.64
  11.3 2.5 %collective-permute-start.5 = (f32[286,2,2]{2,0,1:T(8,128)S(1)}, f32[286,2,2]{2,0,1:T(8,128)S(1)}, u32[]{:S(2)}, u32[]{:S(2)}) collective-permute-start(f32[286,2,2]{2,0,1:T(8,128)S(1)} %get-tuple-element.35), channel_id=1, source_target_pairs={{2,0},{4,2},{6,4},{0,6},{3,1},{5,3},{7,5},{1,7},{10,8},{12,10},{14... | collective-permute-start | bytes 13736 | tf_op jit(solution)/shard_map/ppermute | solution.py:43
  13.9 0.1 select_reduce_fusion
  14.0 0.6 reduce_sum.19
  14.6 1.2 %broadcast_divide_fusion = f32[512]{0:T(512)} fusion(f32[512]{0:T(512)S(1)} %reduce_prod.19, f32[]{:T(128)} %reduce_sum.19), kind=kLoop, calls=%fused_computation.109 | loop fusion | flops 512 | bytes 4100 | tf_op jit(solution)/shard_map/div | solution.py:34
  15.9 0.2 fusion.54
  16.1 3.4 %convolution_reduce_fusion = f32[286,512]{1,0:T(8,128)S(1)} fusion(f32[512,10,4]{0,2,1:T(4,128)S(1)} %fusion.54, s32[286,10]{0,1:T(8,128)} %param.11), kind=kOutput, calls=%fused_computation | convolution fusion | flops 71616688 | bytes 679088 | tf_op jit(solution)/shard_map/qdn,pdn->qpd/dot_general | solution.py:31
  19.5 1.4 %collective-permute-done.5 = f32[286,2,2]{2,0,1:T(8,128)S(1)} collective-permute-done((f32[286,2,2]{2,0,1:T(8,128)S(1)}, f32[286,2,2]{2,0,1:T(8,128)S(1)}, u32[]{:S(2)}, u32[]{:S(2)}) %collective-permute-start.5) | collective-permute-done | bytes 4608 | tf_op jit(solution)/shard_map/ppermute | solution.py:43
  20.9 7.3 %collective-permute-done.4 = f32[286,2,2]{2,0,1:T(8,128)S(1)} collective-permute-done((f32[286,2,2]{2,0,1:T(8,128)S(1)}, f32[286,2,2]{2,0,1:T(8,128)S(1)}, u32[]{:S(2)}, u32[]{:S(2)}) %collective-permute-start.4) | collective-permute-done | bytes 4608 | tf_op jit(solution)/shard_map/ppermute | solution.py:43
  28.3 1.2 %concatenate.47 = f32[286,776]{1,0:T(8,128)} concatenate(f32[286,128]{1,0:T(8,128)S(1)} %get-tuple-element.44, f32[286,128]{1,0:T(8,128)S(1)} %get-tuple-element.43, f32[286,128]{1,0:T(8,128)S(1)} %get-tuple-element.42, f32[286,128]{1,0:T(8,128)S(1)} %get-tuple-element.41, f32[286,128]{1,0:T(8,128)S(1)} %get-tuple-element.40, f32[286,128]{1,0:T(8,128)S(1)} %get-tuple-element.39, ...), dimensions={1} | concatenate | bytes 1775488 | tf_op jit(solution)/shard_map/concatenate | solution.py:75
  29.5 3.9 %fusion.65 = f32[512,776]{0,1:T(8,128)S(1)} fusion(f32[286,512]{1,0:T(8,128)S(1)} %convolution_reduce_fusion, f32[286,776]{1,0:T(8,128)} %concatenate.47), kind=kOutput, calls=%fused_computation.118 | convolution fusion | flops 1363574784 | bytes 3062720 | tf_op jit(solution)/shard_map/dot_general | solution.py:73
  33.5 1.4 %fusion.62 = (f32[512,2,1]{2,1,0:T(2,128)S(1)}, f32[512,2,1]{2,1,0:T(2,128)}) fusion(f32[512,2,128]{2,1,0:T(2,128)S(1)} %bitcast.66), kind=kLoop, calls=%fused_computation.115 | loop fusion | bytes 16384 | tf_op jit(solution)/shard_map/slice | solution.py:57
  34.9 1.2 %copy.97 = f32[512,2,1]{0,2,1:T(1,128)S(1)} copy(f32[512,2,1]{2,1,0:T(2,128)} %get-tuple-element.20) | data formatting | bytes 8192
  36.1 1.5 %collective-permute-start.1 = (f32[512,2,1]{0,2,1:T(1,128)S(1)}, f32[512,2,1]{0,2,1:T(1,128)S(1)}, u32[]{:S(2)}, u32[]{:S(2)}) collective-permute-start(f32[512,2,1]{0,2,1:T(1,128)S(1)} %copy.97), channel_id=1, source_target_pairs={{2,0},{4,2},{6,4},{0,6},{3,1},{5,3},{7,5},{1,7},{10,8},{12,10},{14... | collective-permute-start | bytes 12296 | tf_op jit(solution)/shard_map/ppermute | solution.py:43
  37.6 1.2 %fusion.61 = (f32[512,1,128]{2,1,0:T(1,128)}, f32[512,1,128]{2,1,0:T(1,128)}) fusion(f32[512,2,128]{2,1,0:T(2,128)S(1)} %bitcast.67), kind=kLoop, calls=%fused_computation.114 | loop fusion | bytes 1048576 | tf_op jit(solution)/shard_map/slice | solution.py:60
  38.7 1.1 %copy.96 = f32[512,1,128]{0,2,1:T(8,128)S(1)} copy(f32[512,1,128]{2,1,0:T(1,128)} %get-tuple-element.17) | data formatting | bytes 524288
  39.8 1.1 %copy.98 = f32[512,1,128]{0,2,1:T(8,128)S(1)} copy(f32[512,1,128]{2,1,0:T(1,128)} %get-tuple-element.18) | data formatting | bytes 524288
  41.0 3.5 %collective-permute-start.7 = (f32[512,128]{0,1:T(8,128)S(1)}, f32[512,128]{0,1:T(8,128)}, u32[]{:S(2)}, u32[]{:S(2)}) collective-permute-start(f32[512,128]{0,1:T(8,128)S(1)} %bitcast.68), channel_id=1, source_target_pairs={{1,0},{8,1},{9,8},{16,9},{17,16},{24,17},{25,24},{0,25},{3,2},{10,... | collective-permute-start | bytes 786440 | tf_op jit(solution)/shard_map/ppermute | solution.py:43
  44.5 0.2 copy.95
  44.7 0.6 collective-permute-start
  45.3 3.9 %collective-permute-done = f32[512,2,1]{0,2,1:T(1,128)S(1)} collective-permute-done((f32[512,2,1]{0,2,1:T(1,128)S(1)}, f32[512,2,1]{0,2,1:T(1,128)S(1)}, u32[]{:S(2)}, u32[]{:S(2)}) %collective-permute-start) | collective-permute-done | bytes 4128 | tf_op jit(solution)/shard_map/ppermute | solution.py:43
  49.2 0.1 fusion.19
  49.3 0.5 copy-done.13
  49.8 1.1 %fusion.51 = (f32[512,128]{0,1:T(8,128)S(1)}, f32[512,128]{0,1:T(8,128)S(1)}) fusion(f32[512,776]{0,1:T(8,128)S(1)} %copy-done.1, f32[512,130]{0,1:T(8,128)S(1)} %fusion.19, f32[512,128]{0,1:T(8,128)} %collective-permute-done.6, f32[]{:T(128)S(6)} %select_n.7, f32[512,1,128]{0,2,1:T(8,128)S(1)} %copy.98), kind=kLoop, calls=%fused_computation.70 | loop fusion | flops 720896 | bytes 2621444 | tf_op jit(solution)/shard_map/add | solution.py:89
  51.1 1.2 %fusion.44 = f32[512,128]{0,1:T(8,128)S(1)} fusion(f32[512,776]{0,1:T(8,128)S(1)} %copy-done.1, f32[512,130]{0,1:T(8,128)S(1)} %fusion.21, f32[512,128]{0,1:T(8,128)} %collective-permute-done.7, f32[]{:T(128)S(6)} %select_n.8, f32[512,1,128]{0,2,1:T(8,128)S(1)} %copy.96), kind=kLoop, calls=%fused_computation.60 | loop fusion | flops 720896 | bytes 2097156 | tf_op jit(solution)/shard_map/add | solution.py:89
  52.3 0.7 fusion.2
  53.0 0.2 reshape.17
  53.3 0.1 fusion.63
  53.4 0.1 collective-permute-start.11
  53.5 2.1 %collective-permute-start.9 = (f32[286,2,128]{2,0,1:T(8,128)S(1)}, f32[286,2,128]{2,0,1:T(8,128)S(1)}, u32[]{:S(2)}, u32[]{:S(2)}) collective-permute-start(f32[286,2,128]{2,0,1:T(8,128)S(1)} %fusion.15), channel_id=1, source_target_pairs={{1,0},{8,1},{9,8},{16,9},{17,16},{24,17},{25,24},{0,25},{3,2},{10,... | collective-permute-start | bytes 878600 | tf_op jit(solution)/shard_map/ppermute | solution.py:43
  55.7 1.5 %collective-permute-start.10 = (f32[286,2,2]{2,0,1:T(8,128)S(1)}, f32[286,2,2]{2,0,1:T(8,128)S(1)}, u32[]{:S(2)}, u32[]{:S(2)}) collective-permute-start(f32[286,2,2]{2,0,1:T(8,128)S(1)} %get-tuple-element.24), channel_id=1, source_target_pairs={{0,2},{2,4},{4,6},{6,0},{1,3},{3,5},{5,7},{7,1},{8,10},{10,12},{12... | collective-permute-start | bytes 13736 | tf_op jit(solution)/shard_map/ppermute | solution.py:43
  57.2 6.2 %collective-permute-done.11 = f32[286,2,2]{2,0,1:T(8,128)S(1)} collective-permute-done((f32[286,2,2]{2,0,1:T(8,128)S(1)}, f32[286,2,2]{2,0,1:T(8,128)S(1)}, u32[]{:S(2)}, u32[]{:S(2)}) %collective-permute-start.11) | collective-permute-done | bytes 4608 | tf_op jit(solution)/shard_map/ppermute | solution.py:43
  63.3 6.4 %collective-permute-done.10 = f32[286,2,2]{2,0,1:T(8,128)S(1)} collective-permute-done((f32[286,2,2]{2,0,1:T(8,128)S(1)}, f32[286,2,2]{2,0,1:T(8,128)S(1)}, u32[]{:S(2)}, u32[]{:S(2)}) %collective-permute-start.10) | collective-permute-done | bytes 4608 | tf_op jit(solution)/shard_map/ppermute | solution.py:43
  69.8 0.7 slice_bitcast_fusion.2
  70.5 0.7 slice_bitcast_fusion.4
  71.2 0.7 slice_bitcast_fusion.8
  71.9 1.4 %concatenate.54 = f32[286,776]{1,0:T(8,128)S(1)} concatenate(f32[286,128]{1,0:T(8,128)} %get-tuple-element.32, f32[286,128]{1,0:T(8,128)} %get-tuple-element.31, f32[286,128]{1,0:T(8,128)S(1)} %get-tuple-element.30, f32[286,128]{1,0:T(8,128)S(1)} %get-tuple-element.29, f32[286,128]{1,0:T(8,128)} %get-tuple-element.28, f32[286,128]{1,0:T(8,128)} %get-tuple-element.27, ...), dimensions={1} | concatenate | bytes 1775488 | tf_op jit(solution)/shard_map/concatenate | solution.py:75
  73.3 2.7 %fusion.66 = f32[512,776]{0,1:T(8,128)S(1)} fusion(f32[286,512]{1,0:T(8,128)S(1)} %convolution_reduce_fusion, f32[286,776]{1,0:T(8,128)S(1)} %concatenate.54), kind=kOutput, calls=%fused_computation.119 | convolution fusion | flops 1363574784 | bytes 3062720 | tf_op jit(solution)/shard_map/dot_general | solution.py:73
  76.1 0.1 fusion.23
  76.2 1.1 %fusion.37 = (f32[512,128]{0,1:T(8,128)S(1)}, f32[512,128]{0,1:T(8,128)S(1)}) fusion(f32[512,776]{0,1:T(8,128)S(1)} %fusion.66, f32[512,130]{0,1:T(8,128)S(1)} %fusion.23, f32[512,128]{0,1:T(8,128)} %collective-permute-done.6, f32[]{:T(128)S(6)} %select_n.7, f32[512,1,128]{0,2,1:T(8,128)S(1)} %copy.98), kind=kLoop, calls=%fused_computation.50 | loop fusion | flops 720896 | bytes 2621444 | tf_op jit(solution)/shard_map/add | solution.py:89
  77.5 1.1 %fusion.30 = f32[512,128]{0,1:T(8,128)S(1)} fusion(f32[512,776]{0,1:T(8,128)S(1)} %fusion.66, f32[512,130]{0,1:T(8,128)S(1)} %fusion.25, f32[512,128]{0,1:T(8,128)} %collective-permute-done.7, f32[]{:T(128)S(6)} %select_n.8, f32[512,1,128]{0,2,1:T(8,128)S(1)} %copy.96), kind=kLoop, calls=%fused_computation.40 | loop fusion | flops 720896 | bytes 2097156 | tf_op jit(solution)/shard_map/add | solution.py:89
  78.6 0.7 fusion
  79.3 0.2 reshape.18
  79.5 0.9 %copy.89 = f32[286,2,128]{2,1,0:T(2,128)} copy(f32[286,2,128]{2,0,1:T(8,128)S(1)} %fusion.12) | data formatting | bytes 585728 | tf_op jit(solution)/shard_map/add | solution.py:97
  (68 shorter events, 0.7 us)
Async XLA Ops:
  1.0 27.2 %collective-permute-start.3 = (f32[286,2,128]{2,0,1:T(8,128)S(1)}, f32[286,2,128]{2,0,1:T(8,128)S(1)}, u32[]{:S(2)}, u32[]{:S(2)}) collective-permute-start(f32[286,2,128]{2,0,1:T(8,128)S(1)} %copy.78), channel_id=1, source_target_pairs={{1,0},{8,1},{9,8},{16,9},{17,16},{24,17},{25,24},{0,25},{3,2},{10,... | collective-permute-start | bytes 878600 | tf_op jit(solution)/shard_map/ppermute | solution.py:43
  5.5 22.7 %collective-permute-start.2 = (f32[286,2,128]{2,0,1:T(8,128)S(1)}, f32[286,2,128]{2,0,1:T(8,128)S(1)}, u32[]{:S(2)}, u32[]{:S(2)}) collective-permute-start(f32[286,2,128]{2,0,1:T(8,128)S(1)} %copy.78), channel_id=1, source_target_pairs={{0,1},{1,8},{8,9},{9,16},{16,17},{17,24},{24,25},{25,0},{2,3},{3,1... | collective-permute-start | bytes 878600 | tf_op jit(solution)/shard_map/ppermute | solution.py:43
  7.6 6.3 %copy-start.4 = (s32[512,10]{0,1:T(8,128)S(1)}, s32[512,10]{0,1:T(8,128)}, u32[]{:S(2)}) copy-start(s32[512,10]{0,1:T(8,128)} %param.10) | copy-start | bytes 61444
  7.6 6.3 %copy-start.16 = (f32[4]{0:T(128)S(1)}, f32[4]{0:T(128)}, u32[]{:S(2)}) copy-start(f32[4]{0:T(128)} %constant.42.clone) | copy-start | bytes 52
  7.6 8.3 %copy-start.15 = (f32[4,4,1]{1,0,2:T(4,128)S(1)}, f32[4,4,1]{1,0,2:T(4,128)}, u32[]{:S(2)}) copy-start(f32[4,4,1]{1,0,2:T(4,128)} %constant.56) | copy-start | bytes 196
  7.6 25.9 %all-to-all-start = ((f32[128,4,2,128]{3,2,0,1:T(2,128)}), f32[128,4,2,128]{3,2,0,1:T(2,128)S(1)}, u32[]{:S(2)}, u32[]{:S(2)}) async-start(f32[128,4,2,128]{3,2,0,1:T(2,128)} %copy.67), calls=%async_computation | async-start | bytes 1048576 | tf_op jit(solution)/shard_map/all_to_all | solution.py:54
  11.3 9.5 %collective-permute-start.5 = (f32[286,2,2]{2,0,1:T(8,128)S(1)}, f32[286,2,2]{2,0,1:T(8,128)S(1)}, u32[]{:S(2)}, u32[]{:S(2)}) collective-permute-start(f32[286,2,2]{2,0,1:T(8,128)S(1)} %get-tuple-element.35), channel_id=1, source_target_pairs={{2,0},{4,2},{6,4},{0,6},{3,1},{5,3},{7,5},{1,7},{10,8},{12,10},{14... | collective-permute-start | bytes 13736 | tf_op jit(solution)/shard_map/ppermute | solution.py:43
  13.8 14.3 %collective-permute-start.4 = (f32[286,2,2]{2,0,1:T(8,128)S(1)}, f32[286,2,2]{2,0,1:T(8,128)S(1)}, u32[]{:S(2)}, u32[]{:S(2)}) collective-permute-start(f32[286,2,2]{2,0,1:T(8,128)S(1)} %get-tuple-element.36), channel_id=1, source_target_pairs={{0,2},{2,4},{4,6},{6,0},{1,3},{3,5},{5,7},{7,1},{8,10},{10,12},{12... | collective-permute-start | bytes 13736 | tf_op jit(solution)/shard_map/ppermute | solution.py:43
  33.5 2.6 %copy-start = (f32[512,776]{0,1:T(8,128)}, f32[512,776]{0,1:T(8,128)S(1)}, u32[]{:S(2)}) copy-start(f32[512,776]{0,1:T(8,128)S(1)} %fusion.65) | copy-start | bytes 4767748
  36.1 9.2 %collective-permute-start.1 = (f32[512,2,1]{0,2,1:T(1,128)S(1)}, f32[512,2,1]{0,2,1:T(1,128)S(1)}, u32[]{:S(2)}, u32[]{:S(2)}) collective-permute-start(f32[512,2,1]{0,2,1:T(1,128)S(1)} %copy.97), channel_id=1, source_target_pairs={{2,0},{4,2},{6,4},{0,6},{3,1},{5,3},{7,5},{1,7},{10,8},{12,10},{14... | collective-permute-start | bytes 12296 | tf_op jit(solution)/shard_map/ppermute | solution.py:43
  37.6 11.7 %slice-start = ((f32[512,776]{0,1:T(8,128)}), f32[512,128]{0,1:T(8,128)S(1)}, s32[]{:S(2)}) async-start(f32[512,776]{0,1:T(8,128)} %copy-done), calls=%async_computation.1 | async-start | bytes 524288 | tf_op jit(solution)/shard_map/slice | solution.py:79
  37.6 12.3 %copy-start.1 = (f32[512,776]{0,1:T(8,128)S(1)}, f32[512,776]{0,1:T(8,128)}, u32[]{:S(2)}) copy-start(f32[512,776]{0,1:T(8,128)} %copy-done) | copy-start | bytes 4767748
  40.9 8.9 %collective-permute-start.6 = (f32[512,128]{0,1:T(8,128)S(1)}, f32[512,128]{0,1:T(8,128)}, u32[]{:S(2)}, u32[]{:S(2)}) collective-permute-start(f32[512,128]{0,1:T(8,128)S(1)} %bitcast.71), channel_id=1, source_target_pairs={{0,1},{1,8},{8,9},{9,16},{16,17},{17,24},{24,25},{25,0},{2,3},{3,1... | collective-permute-start | bytes 786440 | tf_op jit(solution)/shard_map/ppermute | solution.py:43
  41.0 10.1 %collective-permute-start.7 = (f32[512,128]{0,1:T(8,128)S(1)}, f32[512,128]{0,1:T(8,128)}, u32[]{:S(2)}, u32[]{:S(2)}) collective-permute-start(f32[512,128]{0,1:T(8,128)S(1)} %bitcast.68), channel_id=1, source_target_pairs={{1,0},{8,1},{9,8},{16,9},{17,16},{24,17},{25,24},{0,25},{3,2},{10,... | collective-permute-start | bytes 786440 | tf_op jit(solution)/shard_map/ppermute | solution.py:43
  44.7 4.5 %collective-permute-start = (f32[512,2,1]{0,2,1:T(1,128)S(1)}, f32[512,2,1]{0,2,1:T(1,128)S(1)}, u32[]{:S(2)}, u32[]{:S(2)}) collective-permute-start(f32[512,2,1]{0,2,1:T(1,128)S(1)} %copy.95), channel_id=1, source_target_pairs={{0,2},{2,4},{4,6},{6,0},{1,3},{3,5},{5,7},{7,1},{8,10},{10,12},{12... | collective-permute-start | bytes 12296 | tf_op jit(solution)/shard_map/ppermute | solution.py:43
  45.3 4.0 %copy-start.11 = (f32[512,1]{0,1:T(1,128)}, f32[512,1]{0,1:T(1,128)S(1)}, u32[]{:S(2)}) copy-start(f32[512,1]{0,1:T(1,128)S(1)} %get-tuple-element.47) | copy-start | bytes 6148
  45.3 5.7 %copy-start.7 = (f32[512,1]{0,1:T(1,128)}, f32[512,1]{0,1:T(1,128)S(1)}, u32[]{:S(2)}) copy-start(f32[512,1]{0,1:T(1,128)S(1)} %get-tuple-element.48) | copy-start | bytes 6148
  49.2 0.6 copy-start.13
  49.2 1.8 %copy-start.9 = (f32[512,1]{0,1:T(1,128)}, f32[512,1]{0,1:T(1,128)S(1)}, u32[]{:S(2)}) copy-start(f32[512,1]{0,1:T(1,128)S(1)} %get-tuple-element.46) | copy-start | bytes 6148
  51.0 1.3 %copy-start.5 = (f32[512]{0:T(512)S(1)}, f32[512]{0:T(512)}, u32[]{:S(2)}) copy-start(f32[512]{0:T(512)} %broadcast_divide_fusion) | copy-start | bytes 6148
  51.1 2.1 %copy-start.2 = (f32[286,2,128]{2,1,0:T(2,128)S(1)}, f32[286,2,128]{2,1,0:T(2,128)}, u32[]{:S(2)}) copy-start(f32[286,2,128]{2,1,0:T(2,128)} %param.7) | copy-start | bytes 878596
  51.1 2.1 %copy-start.3 = (f32[286,2,128]{2,1,0:T(2,128)S(1)}, f32[286,2,128]{2,1,0:T(2,128)}, u32[]{:S(2)}) copy-start(f32[286,2,128]{2,1,0:T(2,128)} %param.8) | copy-start | bytes 878596
  53.4 9.9 %collective-permute-start.11 = (f32[286,2,2]{2,0,1:T(8,128)S(1)}, f32[286,2,2]{2,0,1:T(8,128)S(1)}, u32[]{:S(2)}, u32[]{:S(2)}) collective-permute-start(f32[286,2,2]{2,0,1:T(8,128)S(1)} %get-tuple-element.23), channel_id=1, source_target_pairs={{2,0},{4,2},{6,4},{0,6},{3,1},{5,3},{7,5},{1,7},{10,8},{12,10},{14... | collective-permute-start | bytes 13736 | tf_op jit(solution)/shard_map/ppermute | solution.py:43
  53.5 16.9 %collective-permute-start.9 = (f32[286,2,128]{2,0,1:T(8,128)S(1)}, f32[286,2,128]{2,0,1:T(8,128)S(1)}, u32[]{:S(2)}, u32[]{:S(2)}) collective-permute-start(f32[286,2,128]{2,0,1:T(8,128)S(1)} %fusion.15), channel_id=1, source_target_pairs={{1,0},{8,1},{9,8},{16,9},{17,16},{24,17},{25,24},{0,25},{3,2},{10,... | collective-permute-start | bytes 878600 | tf_op jit(solution)/shard_map/ppermute | solution.py:43
  55.7 15.5 %collective-permute-start.8 = (f32[286,2,128]{2,0,1:T(8,128)S(1)}, f32[286,2,128]{2,0,1:T(8,128)S(1)}, u32[]{:S(2)}, u32[]{:S(2)}) collective-permute-start(f32[286,2,128]{2,0,1:T(8,128)S(1)} %fusion.15), channel_id=1, source_target_pairs={{0,1},{1,8},{8,9},{9,16},{16,17},{17,24},{24,25},{25,0},{2,3},{3,1... | collective-permute-start | bytes 878600 | tf_op jit(solution)/shard_map/ppermute | solution.py:43
  55.7 14.1 %collective-permute-start.10 = (f32[286,2,2]{2,0,1:T(8,128)S(1)}, f32[286,2,2]{2,0,1:T(8,128)S(1)}, u32[]{:S(2)}, u32[]{:S(2)}) collective-permute-start(f32[286,2,2]{2,0,1:T(8,128)S(1)} %get-tuple-element.24), channel_id=1, source_target_pairs={{0,2},{2,4},{4,6},{6,0},{1,3},{3,5},{5,7},{7,1},{8,10},{10,12},{12... | collective-permute-start | bytes 13736 | tf_op jit(solution)/shard_map/ppermute | solution.py:43
  73.3 2.8 %copy-start.12 = (f32[512,1]{0,1:T(1,128)S(1)}, f32[512,1]{0,1:T(1,128)}, u32[]{:S(2)}) copy-start(f32[512,1]{0,1:T(1,128)} %copy-done.11) | copy-start | bytes 6148
  73.3 2.8 %copy-start.14 = (f32[512,1]{0,1:T(1,128)S(1)}, f32[512,1]{0,1:T(1,128)}, u32[]{:S(2)}) copy-start(f32[512,1]{0,1:T(1,128)} %copy-done.13) | copy-start | bytes 6148
  76.1 1.3 %copy-start.8 = (f32[512,1]{0,1:T(1,128)S(1)}, f32[512,1]{0,1:T(1,128)}, u32[]{:S(2)}) copy-start(f32[512,1]{0,1:T(1,128)} %copy-done.7) | copy-start | bytes 6148
  76.1 1.3 %copy-start.10 = (f32[512,1]{0,1:T(1,128)S(1)}, f32[512,1]{0,1:T(1,128)}, u32[]{:S(2)}) copy-start(f32[512,1]{0,1:T(1,128)} %copy-done.9) | copy-start | bytes 6148
  77.4 1.2 %copy-start.6 = (f32[512]{0:T(512)S(1)}, f32[512]{0:T(512)}, u32[]{:S(2)}) copy-start(f32[512]{0:T(512)} %broadcast_divide_fusion) | copy-start | bytes 6148
where the time goes:
time: 81.1 us; the launch traced here: 80.5 us
  waiting for transfers between devices  25.1 us (31%)
  starting transfers between devices  20 us (25%)
  local copies, waits for them, and re-layouts  16.1 us (20%)
  matrix products  11.6 us (14%)
  other arithmetic  7.13 us (9%)
    ppermute x12, waiting for transfers between devices, shift_pair(): return (lax.ppermute(high, axis, up), lax.ppermute(low, axis, down))  25.1 us
    ppermute x12, starting transfers between devices, shift_pair(): return (lax.ppermute(high, axis, up), lax.ppermute(low, axis, down))  16.4 us
    unnamed x40, local copies, waits for them, and re-layouts  7.13 us
    dot_general x2, matrix products, local(): jnp.dot(chaos_basis, jnp.concatenate(parts + edges, 1), precision=top_pre...  6.67 us
    add x4, other arithmetic, local(): (flux_x[:, 2:] - flux_x[:, :-2]) * 0.5 + (flux_y[r + 2] - flux_y[r]) * 0.5  4.61 us
    all_to_all x1, starting transfers between devices, local(): lax.all_to_all(coef_points, 'chaos', split_axis=1, concat_axis=0, tiled=T...  3.6 us
    dot_general x1, matrix products, tables(): factors = jnp.einsum('qdn,pdn->qpd', at_nodes, mode_hot, precision=top_prec)  3.4 us
    concatenate x2, local copies, waits for them, and re-layouts, local(): jnp.concatenate(parts + edges, 1)  2.57 us
  transfers between devices with their start and end apart: 13, of which 5 were waited for; matrix products, arithmetic and copies ran while one was open for 24% of the time, Pallas kernels for 0%

commit v1 on v0

--- a/solution.py
+++ b/solution.py
@@ -10,6 +10,28 @@
 mass_shift = 1.0
 relax_rate = 0.2
 top_prec = lax.Precision.HIGHEST
+
+
+def view_sides_by_axis(field_in, lane_axis, on_dim, join_dim):
+    local_next, carry_out = (jax.lax.psum(1, lane_axis), jax.lax.axis_index(lane_axis))
+    shaped = field_in.shape[on_dim] // local_next
+    r1 = list(field_in.shape)
+    r1[on_dim] = shaped
+    seen_now = r1[join_dim]
+    r1[join_dim] = seen_now * local_next
+    mixed_arr = jnp.zeros(r1, field_in.dtype)
+    d = 0
+    while d < local_next:
+        near = lax.dynamic_slice_in_dim(field_in, (carry_out ^ d) * shaped, shaped, axis=on_dim)
+        if d:
+            near = jax.lax.ppermute(
+                near, lane_axis, [(dev_i, dev_i ^ d) for dev_i in range(local_next)]
+            )
+        mixed_arr = lax.dynamic_update_slice_in_dim(
+            mixed_arr, near, (carry_out ^ d) * seen_now, axis=join_dim
+        )
+        d = d + 1
+    return mixed_arr
 
 
 def tables(quad_index, mode_index):
@@ -51,7 +73,7 @@
     row_devs = lax.axis_size(rows)
     keep_low = jnp.where(row_dev == 0, 0.0, 1.0).astype(jnp.float32)
     keep_high = jnp.where(row_dev == row_devs - 1, 0.0, 1.0).astype(jnp.float32)
-    coef = lax.all_to_all(coef_points, "chaos", split_axis=1, concat_axis=0, tiled=True)
+    coef = view_sides_by_axis(coef_points, "chaos", 1, 0)
     coef = coef.reshape(points, row_len, col_len)
     k_low, k_high = shift_pair(coef[:, 0], coef[:, -1], rows)
     k_left, k_right = shift_pair(coef[:, :, :1], coef[:, :, -1:], "gx")

time: 81.1 us -> 77.7 us (0.958)
  other arithmetic: 7.13 us -> 4.62 us
  matrix products: 11.6 us -> 9.62 us
  waiting for transfers between devices: 25.1 us -> 27 us
  local copies, waits for them, and re-layouts: 16.1 us -> 15.2 us
    ppermute x0 -> x3, waiting for transfers between devices: none -> 5.61 us  [view_sides_by_axis(): jax.lax.ppermute(near, lane_axis, [(dev_i, dev_i ^ d) for dev_i in range(...]
    unnamed x40 -> x20, local copies, waits for them, and re-layouts: 7.13 us -> 2.52 us
    add x4 -> x2, other arithmetic: 4.61 us -> 0.77 us  [local(): (flux_x[:, 2:] - flux_x[:, :-2]) * 0.5 + (flux_y[r + 2] - flux_y[r]) * 0.5]
    ppermute x12, waiting for transfers between devices: 25.1 us -> 21.4 us  [shift_pair(): return (lax.ppermute(high, axis, up), lax.ppermute(low, axis, down))]
    all_to_all x1 -> x0, starting transfers between devices: 3.6 us -> none  [local(): lax.all_to_all(coef_points, 'chaos', split_axis=1, concat_axis=0, tiled=T...]
    ppermute x0 -> x3, starting transfers between devices: none -> 2.92 us  [view_sides_by_axis(): jax.lax.ppermute(near, lane_axis, [(dev_i, dev_i ^ d) for dev_i in range(...]
    squeeze x2, local copies, waits for them, and re-layouts: 0.04 us -> 1.47 us  [local(): v_right[:, r]]
    slice x1, local copies, waits for them, and re-layouts: 1.36 us -> 0.01 us  [local(): k_left, k_right = shift_pair(coef[:, :, :1], coef[:, :, -1:], 'gx')]
  transfers between devices with their start and end apart: 13 -> 15, of which waited for: 5 -> 7; matrix products, arithmetic and copies ran while one was open for 24% -> 24% of each run, Pallas kernels for 0% -> 0%
where the time goes in v1:
time: 77.7 us; the launch traced here: 77.3 us
  waiting for transfers between devices  27 us (35%)
  starting transfers between devices  20.4 us (26%)
  local copies, waits for them, and re-layouts  15.2 us (20%)
  matrix products  9.62 us (12%)
  other arithmetic  4.62 us (6%)
    ppermute x12, waiting for transfers between devices, shift_pair(): return (lax.ppermute(high, axis, up), lax.ppermute(low, axis, down))  21.4 us
    ppermute x12, starting transfers between devices, shift_pair(): return (lax.ppermute(high, axis, up), lax.ppermute(low, axis, down))  17.5 us
    ppermute x3, waiting for transfers between devices, view_sides_by_axis(): jax.lax.ppermute(near, lane_axis, [(dev_i, dev_i ^ d) for dev_i in range(...  5.61 us
    dot_general x2, matrix products, local(): jnp.dot(chaos_basis, jnp.concatenate(parts + edges, 1), precision=top_pre...  5.45 us
    concatenate x2, local copies, waits for them, and re-layouts, local(): jnp.concatenate(parts + edges, 1)  3.07 us
    ppermute x3, starting transfers between devices, view_sides_by_axis(): jax.lax.ppermute(near, lane_axis, [(dev_i, dev_i ^ d) for dev_i in range(...  2.92 us
    dot_general x1, matrix products, tables(): factors = jnp.einsum('qdn,pdn->qpd', at_nodes, mode_hot, precision=top_prec)  2.62 us
    unnamed x20, local copies, waits for them, and re-layouts  2.52 us
  transfers between devices with their start and end apart: 15, of which 7 were waited for; matrix products, arithmetic and copies ran while one was open for 24% of the time, Pallas kernels for 0%

profile of v1, /device:TPU:0, one launch (start us, length us, event | category | flops | bytes accessed | tf_op | source)
XLA Modules:
  0.0 77.3 jit_solution(10257930722334462012)
XLA Ops:
  0.0 1.0 %copy.63 = f32[286,2,128]{2,0,1:T(8,128)S(1)} copy(f32[286,2,128]{2,1,0:T(2,128)} %param.7) | data formatting | bytes 585728 | tf_op args[0]
  1.0 4.5 %collective-permute-start.6 = (f32[286,2,128]{2,0,1:T(8,128)S(1)}, f32[286,2,128]{2,0,1:T(8,128)}, u32[]{:S(2)}, u32[]{:S(2)}) collective-permute-start(f32[286,2,128]{2,0,1:T(8,128)S(1)} %copy.63), channel_id=1, source_target_pairs={{1,0},{8,1},{9,8},{16,9},{17,16},{24,17},{25,24},{0,25},{3,2},{10,... | collective-permute-start | bytes 878600 | tf_op jit(solution)/shard_map/ppermute | solution.py:65
  5.5 1.2 %constant_dynamic-slice_fusion = (f32[128,1,2,128]{3,2,1,0:T(2,128)S(1)}, f32[128,1,2,128]{3,2,1,0:T(2,128)S(1)}, f32[128,1,2,128]{3,2,1,0:T(2,128)S(1)}, f32[128,1,2,128]{3,2,1,0:T(2,128)S(1)}) fusion(f32[128,4,2,128]{3,2,1,0:T(2,128)} %param.9, s32[]{:T(128)S(6)} %select_n.37, s32[]{:T(128)S(6)} %select_n.35, s32[]{:T(128)S(6)} %select_n.33, s32[]{:T(128)S(6)} %select_n.31), kind=kLoop, calls=%fused_computation.115 | loop fusion | bytes 1048592 | tf_op jit(solution)/shard_map/dynamic_slice | solution.py:25
  7.0 1.7 %collective-permute-start.1 = (f32[128,1,2,128]{0,3,2,1:T(8,128)S(1)}, f32[128,1,2,128]{0,3,2,1:T(8,128)S(1)}, u32[]{:S(2)}, u32[]{:S(2)}) collective-permute-start(f32[128,1,2,128]{0,3,2,1:T(8,128)S(1)} %copy.80), channel_id=1, source_target_pairs={{0,16},{8,24},{16,0},{24,8},{1,17},{9,25},{17,1},{25,9},{2,18},{10... | collective-permute-start | bytes 393224 | tf_op jit(solution)/shard_map/ppermute | solution.py:27
  8.8 2.5 %collective-permute-start.8 = (f32[286,2,2]{2,0,1:T(8,128)S(1)}, f32[286,2,2]{2,0,1:T(8,128)S(1)}, u32[]{:S(2)}, u32[]{:S(2)}) collective-permute-start(f32[286,2,2]{2,0,1:T(8,128)S(1)} %get-tuple-element.43), channel_id=1, source_target_pairs={{2,0},{4,2},{6,4},{0,6},{3,1},{5,3},{7,5},{1,7},{10,8},{12,10},{14... | collective-permute-start | bytes 13736 | tf_op jit(solution)/shard_map/ppermute | solution.py:65
  11.5 0.6 reduce_sum.19
  12.1 0.6 broadcast_divide_fusion
  12.8 0.2 fusion.54
  13.2 2.6 %convolution_reduce_fusion = f32[286,512]{1,0:T(8,128)S(1)} fusion(f32[512,10,4]{0,2,1:T(4,128)S(1)} %fusion.54, s32[286,10]{0,1:T(8,128)S(1)} %copy-done.7), kind=kOutput, calls=%fused_computation | convolution fusion | flops 71616688 | bytes 679088 | tf_op jit(solution)/shard_map/qdn,pdn->qpd/dot_general | solution.py:53
  16.0 1.4 %collective-permute-done.8 = f32[286,2,2]{2,0,1:T(8,128)S(1)} collective-permute-done((f32[286,2,2]{2,0,1:T(8,128)S(1)}, f32[286,2,2]{2,0,1:T(8,128)S(1)}, u32[]{:S(2)}, u32[]{:S(2)}) %collective-permute-start.8) | collective-permute-done | bytes 4608 | tf_op jit(solution)/shard_map/ppermute | solution.py:65
  17.4 2.4 %collective-permute-start.7 = (f32[286,2,2]{2,0,1:T(8,128)S(1)}, f32[286,2,2]{2,0,1:T(8,128)S(1)}, u32[]{:S(2)}, u32[]{:S(2)}) collective-permute-start(f32[286,2,2]{2,0,1:T(8,128)S(1)} %get-tuple-element.44), channel_id=1, source_target_pairs={{0,2},{2,4},{4,6},{6,0},{1,3},{3,5},{5,7},{7,1},{8,10},{10,12},{12... | collective-permute-start | bytes 13736 | tf_op jit(solution)/shard_map/ppermute | solution.py:65
  19.8 0.7 slice_bitcast_fusion.12
  20.5 7.6 %collective-permute-done.7 = f32[286,2,2]{2,0,1:T(8,128)S(1)} collective-permute-done((f32[286,2,2]{2,0,1:T(8,128)S(1)}, f32[286,2,2]{2,0,1:T(8,128)S(1)}, u32[]{:S(2)}, u32[]{:S(2)}) %collective-permute-start.7) | collective-permute-done | bytes 4608 | tf_op jit(solution)/shard_map/ppermute | solution.py:65
  28.2 1.2 %collective-permute-start.2 = (f32[128,1,2,128]{0,3,2,1:T(8,128)S(1)}, f32[128,1,2,128]{0,3,2,1:T(8,128)S(1)}, u32[]{:S(2)}, u32[]{:S(2)}) collective-permute-start(f32[128,1,2,128]{0,3,2,1:T(8,128)S(1)} %copy.81), channel_id=1, source_target_pairs={{0,24},{8,16},{16,8},{24,0},{1,25},{9,17},{17,9},{25,1},{2,26},{10... | collective-permute-start | bytes 393224 | tf_op jit(solution)/shard_map/ppermute | solution.py:27
  29.3 0.7 slice_bitcast_fusion.14
  30.1 5.6 %collective-permute-done.2 = f32[128,1,2,128]{0,3,2,1:T(8,128)S(1)} collective-permute-done((f32[128,1,2,128]{0,3,2,1:T(8,128)S(1)}, f32[128,1,2,128]{0,3,2,1:T(8,128)S(1)}, u32[]{:S(2)}, u32[]{:S(2)}) %collective-permute-start.2) | collective-permute-done | bytes 131104 | tf_op jit(solution)/shard_map/ppermute | solution.py:27
  35.8 1.2 %collective-permute-start.3 = (f32[512,2,1]{0,2,1:T(1,128)S(1)}, f32[512,2,1]{0,2,1:T(1,128)S(1)}, u32[]{:S(2)}, u32[]{:S(2)}) collective-permute-start(f32[512,2,1]{0,2,1:T(1,128)S(1)} %get-tuple-element.23), channel_id=1, source_target_pairs={{0,2},{2,4},{4,6},{6,0},{1,3},{3,5},{5,7},{7,1},{8,10},{10,12},{12... | collective-permute-start | bytes 12296 | tf_op jit(solution)/shard_map/ppermute | solution.py:65
  37.0 1.9 %collective-permute-start.4 = (f32[512,2,1]{0,2,1:T(1,128)S(1)}, f32[512,2,1]{0,2,1:T(1,128)S(1)}, u32[]{:S(2)}, u32[]{:S(2)}) collective-permute-start(f32[512,2,1]{0,2,1:T(1,128)S(1)} %get-tuple-element.24), channel_id=1, source_target_pairs={{2,0},{4,2},{6,4},{0,6},{3,1},{5,3},{7,5},{1,7},{10,8},{12,10},{14... | collective-permute-start | bytes 12296 | tf_op jit(solution)/shard_map/ppermute | solution.py:65
  38.8 1.5 %collective-permute-done.3 = f32[512,2,1]{0,2,1:T(1,128)S(1)} collective-permute-done((f32[512,2,1]{0,2,1:T(1,128)S(1)}, f32[512,2,1]{0,2,1:T(1,128)S(1)}, u32[]{:S(2)}, u32[]{:S(2)}) %collective-permute-start.3) | collective-permute-done | bytes 4128 | tf_op jit(solution)/shard_map/ppermute | solution.py:65
  40.3 0.3 collective-permute-done.4
  40.6 1.0 %broadcast_multiply_fusion.1 = f32[286,2,128]{2,0,1:T(8,128)S(1)} fusion(f32[286,2,128]{2,0,1:T(8,128)} %collective-permute-done.6, f32[]{:T(128)S(6)} %select_n.40), kind=kLoop, calls=%fused_computation.98 | loop fusion | flops 73216 | bytes 585732 | tf_op jit(solution)/shard_map/mul | solution.py:88
  41.6 0.7 slice_bitcast_fusion.16
  42.4 1.0 %broadcast_multiply_fusion.3 = f32[286,2,128]{2,0,1:T(8,128)S(1)} fusion(f32[286,2,128]{2,0,1:T(8,128)} %collective-permute-done.5, f32[]{:T(128)S(6)} %select_n.39), kind=kLoop, calls=%fused_computation.100 | loop fusion | flops 73216 | bytes 585732 | tf_op jit(solution)/shard_map/mul | solution.py:87
  43.3 0.7 slice_bitcast_fusion.20
  44.1 1.5 %concatenate.47 = f32[286,776]{1,0:T(8,128)S(1)} concatenate(f32[286,128]{1,0:T(8,128)} %get-tuple-element.52, f32[286,128]{1,0:T(8,128)} %get-tuple-element.51, f32[286,128]{1,0:T(8,128)S(1)} %get-tuple-element.50, f32[286,128]{1,0:T(8,128)S(1)} %get-tuple-element.49, f32[286,128]{1,0:T(8,128)} %get-tuple-element.48, f32[286,128]{1,0:T(8,128)} %get-tuple-element.47, ...), dimensions={1} | concatenate | bytes 1775488 | tf_op jit(solution)/shard_map/concatenate | solution.py:97
  45.6 2.7 %fusion.66 = f32[512,776]{0,1:T(8,128)S(1)} fusion(f32[286,512]{1,0:T(8,128)S(1)} %convolution_reduce_fusion, f32[286,776]{1,0:T(8,128)S(1)} %concatenate.47), kind=kOutput, calls=%fused_computation.129 | convolution fusion | flops 1363574784 | bytes 3062720 | tf_op jit(solution)/shard_map/dot_general | solution.py:95
  48.3 0.2 fusion.19
  48.5 0.4 fusion.51
  48.9 0.3 copy-done.2
  49.2 0.7 fusion.2
  49.9 0.2 reshape.36
  50.5 2.8 %collective-permute-start.14 = (f32[286,2,2]{2,0,1:T(8,128)S(1)}, f32[286,2,2]{2,0,1:T(8,128)S(1)}, u32[]{:S(2)}, u32[]{:S(2)}) collective-permute-start(f32[286,2,2]{2,0,1:T(8,128)S(1)} %get-tuple-element.31), channel_id=1, source_target_pairs={{2,0},{4,2},{6,4},{0,6},{3,1},{5,3},{7,5},{1,7},{10,8},{12,10},{14... | collective-permute-start | bytes 13736 | tf_op jit(solution)/shard_map/ppermute | solution.py:65
  53.2 0.7 slice_bitcast_fusion.8
  54.0 1.4 %collective-permute-start.12 = (f32[286,2,128]{2,0,1:T(8,128)S(1)}, f32[286,2,128]{2,0,1:T(8,128)S(1)}, u32[]{:S(2)}, u32[]{:S(2)}) collective-permute-start(f32[286,2,128]{2,0,1:T(8,128)S(1)} %fusion.15), channel_id=1, source_target_pairs={{1,0},{8,1},{9,8},{16,9},{17,16},{24,17},{25,24},{0,25},{3,2},{10,... | collective-permute-start | bytes 878600 | tf_op jit(solution)/shard_map/ppermute | solution.py:65
  55.4 0.8 %collective-permute-start.13 = (f32[286,2,2]{2,0,1:T(8,128)S(1)}, f32[286,2,2]{2,0,1:T(8,128)S(1)}, u32[]{:S(2)}, u32[]{:S(2)}) collective-permute-start(f32[286,2,2]{2,0,1:T(8,128)S(1)} %get-tuple-element.32), channel_id=1, source_target_pairs={{0,2},{2,4},{4,6},{6,0},{1,3},{3,5},{5,7},{7,1},{8,10},{10,12},{12... | collective-permute-start | bytes 13736 | tf_op jit(solution)/shard_map/ppermute | solution.py:65
  56.3 4.5 %collective-permute-done.14 = f32[286,2,2]{2,0,1:T(8,128)S(1)} collective-permute-done((f32[286,2,2]{2,0,1:T(8,128)S(1)}, f32[286,2,2]{2,0,1:T(8,128)S(1)}, u32[]{:S(2)}, u32[]{:S(2)}) %collective-permute-start.14) | collective-permute-done | bytes 4608 | tf_op jit(solution)/shard_map/ppermute | solution.py:65
  60.8 0.7 slice_bitcast_fusion.2
  61.5 6.0 %collective-permute-done.13 = f32[286,2,2]{2,0,1:T(8,128)S(1)} collective-permute-done((f32[286,2,2]{2,0,1:T(8,128)S(1)}, f32[286,2,2]{2,0,1:T(8,128)S(1)}, u32[]{:S(2)}, u32[]{:S(2)}) %collective-permute-start.13) | collective-permute-done | bytes 4608 | tf_op jit(solution)/shard_map/ppermute | solution.py:65
  67.5 0.7 slice_bitcast_fusion.4
  68.3 0.7 slice_bitcast_fusion.6
  69.1 0.7 slice_bitcast_fusion.10
  69.8 1.6 %concatenate.54 = f32[286,776]{1,0:T(8,128)S(1)} concatenate(f32[286,128]{1,0:T(8,128)} %get-tuple-element.40, f32[286,128]{1,0:T(8,128)} %get-tuple-element.39, f32[286,128]{1,0:T(8,128)} %get-tuple-element.38, f32[286,128]{1,0:T(8,128)} %get-tuple-element.37, f32[286,128]{1,0:T(8,128)} %get-tuple-element.36, f32[286,128]{1,0:T(8,128)} %get-tuple-element.35, ...), dimensions={1} | concatenate | bytes 1775488 | tf_op jit(solution)/shard_map/concatenate | solution.py:97
  71.4 2.7 %fusion.67 = f32[512,776]{0,1:T(8,128)S(1)} fusion(f32[286,512]{1,0:T(8,128)S(1)} %convolution_reduce_fusion, f32[286,776]{1,0:T(8,128)S(1)} %concatenate.54), kind=kOutput, calls=%fused_computation.130 | convolution fusion | flops 1363574784 | bytes 3062720 | tf_op jit(solution)/shard_map/dot_general | solution.py:95
  74.4 0.7 copy-done.3
  75.1 0.4 fusion.37
  75.5 0.7 fusion
  76.1 0.2 reshape.37
  76.4 0.9 %copy.74 = f32[286,2,128]{2,1,0:T(2,128)} copy(f32[286,2,128]{2,0,1:T(8,128)S(1)} %fusion.12) | data formatting | bytes 585728 | tf_op jit(solution)/shard_map/add | solution.py:119
  (55 shorter events, 1.7 us)
Async XLA Ops:
  1.0 39.7 %collective-permute-start.6 = (f32[286,2,128]{2,0,1:T(8,128)S(1)}, f32[286,2,128]{2,0,1:T(8,128)}, u32[]{:S(2)}, u32[]{:S(2)}) collective-permute-start(f32[286,2,128]{2,0,1:T(8,128)S(1)} %copy.63), channel_id=1, source_target_pairs={{1,0},{8,1},{9,8},{16,9},{17,16},{24,17},{25,24},{0,25},{3,2},{10,... | collective-permute-start | bytes 878600 | tf_op jit(solution)/shard_map/ppermute | solution.py:65
  5.5 36.8 %collective-permute-start.5 = (f32[286,2,128]{2,0,1:T(8,128)S(1)}, f32[286,2,128]{2,0,1:T(8,128)}, u32[]{:S(2)}, u32[]{:S(2)}) collective-permute-start(f32[286,2,128]{2,0,1:T(8,128)S(1)} %copy.63), channel_id=1, source_target_pairs={{0,1},{1,8},{8,9},{9,16},{16,17},{17,24},{24,25},{25,0},{2,3},{3,1... | collective-permute-start | bytes 878600 | tf_op jit(solution)/shard_map/ppermute | solution.py:65
  5.5 5.8 %copy-start.4 = (s32[512,10]{0,1:T(8,128)S(1)}, s32[512,10]{0,1:T(8,128)}, u32[]{:S(2)}) copy-start(s32[512,10]{0,1:T(8,128)} %param.10) | copy-start | bytes 61444
  5.5 5.8 %copy-start.6 = (f32[4]{0:T(128)S(1)}, f32[4]{0:T(128)}, u32[]{:S(2)}) copy-start(f32[4]{0:T(128)} %constant.57.clone) | copy-start | bytes 52
  5.5 7.3 %copy-start.5 = (f32[4,4,1]{1,0,2:T(4,128)S(1)}, f32[4,4,1]{1,0,2:T(4,128)}, u32[]{:S(2)}) copy-start(f32[4,4,1]{1,0,2:T(4,128)} %constant.71) | copy-start | bytes 196
  6.8 23.2 %collective-permute-start = (f32[128,1,2,128]{0,3,2,1:T(8,128)S(1)}, f32[128,1,2,128]{0,3,2,1:T(8,128)S(1)}, u32[]{:S(2)}, u32[]{:S(2)}) collective-permute-start(f32[128,1,2,128]{0,3,2,1:T(8,128)S(1)} %copy.79), channel_id=1, source_target_pairs={{0,8},{8,0},{16,24},{24,16},{1,9},{9,1},{17,25},{25,17},{2,10},{10... | collective-permute-start | bytes 393224 | tf_op jit(solution)/shard_map/ppermute | solution.py:27
  7.0 6.2 %copy-start.7 = (s32[286,10]{0,1:T(8,128)S(1)}, s32[286,10]{0,1:T(8,128)}, u32[]{:S(2)}) copy-start(s32[286,10]{0,1:T(8,128)} %param.11) | copy-start | bytes 34324
  7.0 23.1 %collective-permute-start.1 = (f32[128,1,2,128]{0,3,2,1:T(8,128)S(1)}, f32[128,1,2,128]{0,3,2,1:T(8,128)S(1)}, u32[]{:S(2)}, u32[]{:S(2)}) collective-permute-start(f32[128,1,2,128]{0,3,2,1:T(8,128)S(1)} %copy.80), channel_id=1, source_target_pairs={{0,16},{8,24},{16,0},{24,8},{1,17},{9,25},{17,1},{25,9},{2,18},{10... | collective-permute-start | bytes 393224 | tf_op jit(solution)/shard_map/ppermute | solution.py:27
  8.8 8.6 %collective-permute-start.8 = (f32[286,2,2]{2,0,1:T(8,128)S(1)}, f32[286,2,2]{2,0,1:T(8,128)S(1)}, u32[]{:S(2)}, u32[]{:S(2)}) collective-permute-start(f32[286,2,2]{2,0,1:T(8,128)S(1)} %get-tuple-element.43), channel_id=1, source_target_pairs={{2,0},{4,2},{6,4},{0,6},{3,1},{5,3},{7,5},{1,7},{10,8},{12,10},{14... | collective-permute-start | bytes 13736 | tf_op jit(solution)/shard_map/ppermute | solution.py:65
  17.4 10.8 %collective-permute-start.7 = (f32[286,2,2]{2,0,1:T(8,128)S(1)}, f32[286,2,2]{2,0,1:T(8,128)S(1)}, u32[]{:S(2)}, u32[]{:S(2)}) collective-permute-start(f32[286,2,2]{2,0,1:T(8,128)S(1)} %get-tuple-element.44), channel_id=1, source_target_pairs={{0,2},{2,4},{4,6},{6,0},{1,3},{3,5},{5,7},{7,1},{8,10},{10,12},{12... | collective-permute-start | bytes 13736 | tf_op jit(solution)/shard_map/ppermute | solution.py:65
  28.2 7.6 %collective-permute-start.2 = (f32[128,1,2,128]{0,3,2,1:T(8,128)S(1)}, f32[128,1,2,128]{0,3,2,1:T(8,128)S(1)}, u32[]{:S(2)}, u32[]{:S(2)}) collective-permute-start(f32[128,1,2,128]{0,3,2,1:T(8,128)S(1)} %copy.81), channel_id=1, source_target_pairs={{0,24},{8,16},{16,8},{24,0},{1,25},{9,17},{17,9},{25,1},{2,26},{10... | collective-permute-start | bytes 393224 | tf_op jit(solution)/shard_map/ppermute | solution.py:27
  35.8 4.6 %collective-permute-start.3 = (f32[512,2,1]{0,2,1:T(1,128)S(1)}, f32[512,2,1]{0,2,1:T(1,128)S(1)}, u32[]{:S(2)}, u32[]{:S(2)}) collective-permute-start(f32[512,2,1]{0,2,1:T(1,128)S(1)} %get-tuple-element.23), channel_id=1, source_target_pairs={{0,2},{2,4},{4,6},{6,0},{1,3},{3,5},{5,7},{7,1},{8,10},{10,12},{12... | collective-permute-start | bytes 12296 | tf_op jit(solution)/shard_map/ppermute | solution.py:65
  37.0 3.7 %collective-permute-start.4 = (f32[512,2,1]{0,2,1:T(1,128)S(1)}, f32[512,2,1]{0,2,1:T(1,128)S(1)}, u32[]{:S(2)}, u32[]{:S(2)}) collective-permute-start(f32[512,2,1]{0,2,1:T(1,128)S(1)} %get-tuple-element.24), channel_id=1, source_target_pairs={{2,0},{4,2},{6,4},{0,6},{3,1},{5,3},{7,5},{1,7},{10,8},{12,10},{14... | collective-permute-start | bytes 12296 | tf_op jit(solution)/shard_map/ppermute | solution.py:65
  38.8 9.7 %collective-permute-start.10 = (f32[512,128]{0,1:T(8,128)S(1)}, f32[512,128]{0,1:T(8,128)S(1)}, u32[]{:S(2)}, u32[]{:S(2)}) collective-permute-start(f32[512,128]{0,1:T(8,128)S(1)} %get-tuple-element.21), channel_id=1, source_target_pairs={{1,0},{8,1},{9,8},{16,9},{17,16},{24,17},{25,24},{0,25},{3,2},{10,... | collective-permute-start | bytes 786440 | tf_op jit(solution)/shard_map/ppermute | solution.py:65
  40.3 8.2 %collective-permute-start.9 = (f32[512,128]{0,1:T(8,128)S(1)}, f32[512,128]{0,1:T(8,128)S(1)}, u32[]{:S(2)}, u32[]{:S(2)}) collective-permute-start(f32[512,128]{0,1:T(8,128)S(1)} %get-tuple-element.22), channel_id=1, source_target_pairs={{0,1},{1,8},{8,9},{9,16},{16,17},{17,24},{24,25},{25,0},{2,3},{3,1... | collective-permute-start | bytes 786440 | tf_op jit(solution)/shard_map/ppermute | solution.py:65
  48.5 0.7 copy-start.2
  49.2 1.0 %copy-start = (f32[286,2,128]{2,1,0:T(2,128)S(1)}, f32[286,2,128]{2,1,0:T(2,128)}, u32[]{:S(2)}) copy-start(f32[286,2,128]{2,1,0:T(2,128)} %param.7) | copy-start | bytes 878596
  49.2 1.0 %copy-start.1 = (f32[286,2,128]{2,1,0:T(2,128)S(1)}, f32[286,2,128]{2,1,0:T(2,128)}, u32[]{:S(2)}) copy-start(f32[286,2,128]{2,1,0:T(2,128)} %param.8) | copy-start | bytes 878596
  50.5 10.3 %collective-permute-start.14 = (f32[286,2,2]{2,0,1:T(8,128)S(1)}, f32[286,2,2]{2,0,1:T(8,128)S(1)}, u32[]{:S(2)}, u32[]{:S(2)}) collective-permute-start(f32[286,2,2]{2,0,1:T(8,128)S(1)} %get-tuple-element.31), channel_id=1, source_target_pairs={{2,0},{4,2},{6,4},{0,6},{3,1},{5,3},{7,5},{1,7},{10,8},{12,10},{14... | collective-permute-start | bytes 13736 | tf_op jit(solution)/shard_map/ppermute | solution.py:65
  54.0 14.3 %collective-permute-start.12 = (f32[286,2,128]{2,0,1:T(8,128)S(1)}, f32[286,2,128]{2,0,1:T(8,128)S(1)}, u32[]{:S(2)}, u32[]{:S(2)}) collective-permute-start(f32[286,2,128]{2,0,1:T(8,128)S(1)} %fusion.15), channel_id=1, source_target_pairs={{1,0},{8,1},{9,8},{16,9},{17,16},{24,17},{25,24},{0,25},{3,2},{10,... | collective-permute-start | bytes 878600 | tf_op jit(solution)/shard_map/ppermute | solution.py:65
  55.4 13.6 %collective-permute-start.11 = (f32[286,2,128]{2,0,1:T(8,128)S(1)}, f32[286,2,128]{2,0,1:T(8,128)S(1)}, u32[]{:S(2)}, u32[]{:S(2)}) collective-permute-start(f32[286,2,128]{2,0,1:T(8,128)S(1)} %fusion.15), channel_id=1, source_target_pairs={{0,1},{1,8},{8,9},{9,16},{16,17},{17,24},{24,25},{25,0},{2,3},{3,1... | collective-permute-start | bytes 878600 | tf_op jit(solution)/shard_map/ppermute | solution.py:65
  55.4 12.1 %collective-permute-start.13 = (f32[286,2,2]{2,0,1:T(8,128)S(1)}, f32[286,2,2]{2,0,1:T(8,128)S(1)}, u32[]{:S(2)}, u32[]{:S(2)}) collective-permute-start(f32[286,2,2]{2,0,1:T(8,128)S(1)} %get-tuple-element.32), channel_id=1, source_target_pairs={{0,2},{2,4},{4,6},{6,0},{1,3},{3,5},{5,7},{7,1},{8,10},{10,12},{12... | collective-permute-start | bytes 13736 | tf_op jit(solution)/shard_map/ppermute | solution.py:65
  74.1 1.0 %copy-start.3 = (f32[512,128]{0,1:T(8,128)S(1)}, f32[512,128]{0,1:T(8,128)}, u32[]{:S(2)}) copy-start(f32[512,128]{0,1:T(8,128)} %copy-done.2) | copy-start | bytes 786436
